TPU v7x, 32 devices: a whole 2x2x4 slice. The times are simulated.
32 devices in a mesh: py: 4 (over y, x), pz: 8 (over z, core).
Axes of the slice: x: 2, y: 2, z: 4, core: 2. Of those that a mesh axis runs over, the one named last changes fastest.
Arguments:
- field_one: float32 [256, 256, 512], P('py', 'pz'), may hold values from -6 to 6
- field_two: float32 [256, 256, 512], P('py', 'pz'), may hold values from -6 to 6
- coef: float32 [2, 2, 8], replicated, may hold values from -4 to 4
Outputs:
- potential_one: float32 [256, 256, 512], P('py', 'pz')
- potential_two: float32 [256, 256, 512], P('py', 'pz')
All inputs are finite; a program needn't handle non-finite values.
Results may differ from a plain program's by a relative error of at most 0.00013.
Values sent between devices are 32-bit elements; how exact they have to be, the bound alone decides.
No kernel may reach another device: no remote copies, remote signals or barrier semaphores. Data moves between devices by JAX's collectives and lax.ppermute only.
A program may use at most 256 MiB of HBM per device.

v0:
```python
import math
import jax
import jax.numpy as jnp
from jax import lax
from jax.sharding import PartitionSpec as P

HIGH = lax.Precision.HIGHEST


def padded_2(value, sides, width):
    for axis, dim in sides:
        size, length = (lax.axis_size(axis), value.shape[dim])
        up = [(i, (i + 1) % size) for i in range(size)]
        down = [(j, i) for i, j in up]
        last = lax.slice_in_dim(value, length - width, length, axis=dim)
        leading = lax.slice_in_dim(value, 0, width, axis=dim)
        before = lax.ppermute(last, axis, up)
        after = lax.ppermute(leading, axis, down)
        value = jnp.concatenate([before, value, after], axis=dim)
    return value


def freq_at(position, length):
    paired = position // 2
    odd_bit = position % 2
    inner = jnp.where(odd_bit == 0, paired, length - paired)
    return jnp.where(paired == 0, odd_bit * (length // 2), inner)


def scaled_signed(freq, length):
    return jnp.where(freq > length // 2, freq - length, freq).astype(jnp.float32) / length


def forward_table(length):
    indices = jnp.arange(length, dtype=jnp.int32)
    freq = freq_at(indices, length)
    phase = indices[:, None] * freq[None, :] % length
    angle = 2.0 * math.pi / length * phase.astype(jnp.float32)
    return (jnp.cos(angle), jnp.sin(angle))


def inverse_table(length):
    cosine, sine = forward_table(length)
    return (cosine.T / length, sine.T / length)


def contract(form, data, table):
    return jnp.einsum(form, data, table, precision=HIGH)


def complex_apply(form, real_part, imag_part, cosine, sine, sign):
    if imag_part is None:
        return (contract(form, real_part, cosine), -sign * contract(form, real_part, sine))
    real_out = contract(form, real_part, cosine) + sign * contract(form, imag_part, sine)
    imag_out = contract(form, imag_part, cosine) - sign * contract(form, real_part, sine)
    return (real_out, imag_out)


def make_kernel(coef, freqs, lengths):
    radius = scaled_signed(freqs[0], lengths[0]) ** 2 + scaled_signed(freqs[1], lengths[1]) ** 2
    radius = radius + scaled_signed(freqs[2], lengths[2]) ** 2
    ratio = 4.0 * radius / 3.0
    volume = ratio * jnp.sqrt(ratio)
    basis_count = coef.shape[2]
    centres = (jnp.arange(basis_count, dtype=jnp.float32) + 0.5) / basis_count
    basis = jnp.exp(-jnp.square((volume[None] - centres[:, None, None, None]) * basis_count))
    kernel = jnp.einsum("abr,rkxm->abkxm", coef, basis, precision=HIGH)
    return kernel


def shards(field_one, field_two, coef):
    y_local, z_local, x_count = field_one.shape
    py_count = lax.axis_size("py")
    pz_count = lax.axis_size("pz")
    y_count = y_local * py_count
    z_count = z_local * pz_count
    x_block = x_count // py_count
    ky_block = y_count // pz_count
    cells = y_local * z_local
    fields = jnp.stack([field_one, field_two])
    along_x = (4.0 * fields + jnp.roll(fields, 1, 3) + jnp.roll(fields, -1, 3)) / 6.0
    padded = padded_2(along_x, (("py", 1), ("pz", 2)), 1)
    along_y = (4.0 * padded[:, 1:-1] + padded[:, 2:] + padded[:, :-2]) / 6.0
    smoothed = (4.0 * along_y[:, :, 1:-1] + along_y[:, :, 2:] + along_y[:, :, :-2]) / 6.0
    flat = smoothed.reshape(2, cells, x_count)
    x_cos, x_sin = forward_table(x_count)
    real_part, imag_part = complex_apply("bsx,xq->bqs", flat, None, x_cos, x_sin, 1.0)
    batch = real_part.shape[0]
    y_cos, y_sin = forward_table(y_count)
    z_cos, z_sin = forward_table(z_count)
    zi_cos, zi_sin = inverse_table(z_count)
    yi_cos, yi_sin = inverse_table(y_count)
    xi_cos, xi_sin = inverse_table(x_count)
    real_in = lax.all_to_all(real_part, "py", split_axis=1, concat_axis=2, tiled=True)
    imag_in = lax.all_to_all(imag_part, "py", split_axis=1, concat_axis=2, tiled=True)
    items = real_in.shape[0]

    def relay(values):
        values = values.reshape(items, x_block, y_count, z_local).transpose(0, 2, 1, 3)
        return values.reshape(items, y_count, x_block * z_local)

    real_part, imag_part = complex_apply(
        "byc,yk->bkc", relay(real_in), relay(imag_in), y_cos, y_sin, 1.0
    )
    real_in = lax.all_to_all(real_part, "pz", split_axis=1, concat_axis=2, tiled=True)
    imag_in = lax.all_to_all(imag_part, "pz", split_axis=1, concat_axis=2, tiled=True)
    lines_items = real_in.shape[0]

    def relay(values):
        values = values.reshape(lines_items, ky_block, pz_count, x_block, z_local).transpose(
            0, 1, 3, 2, 4
        )
        return values.reshape(lines_items, ky_block, x_block, z_count)

    real_part, imag_part = complex_apply(
        "bkxz,zm->bkxm", relay(real_in), relay(imag_in), z_cos, z_sin, 1.0
    )
    ky_start = lax.axis_index("pz") * ky_block
    kx_start = lax.axis_index("py") * x_block
    freq_y = freq_at(ky_start + jnp.arange(ky_block, dtype=jnp.int32), y_count)
    freq_x = freq_at(kx_start + jnp.arange(x_block, dtype=jnp.int32), x_count)
    freq_z = freq_at(jnp.arange(z_count, dtype=jnp.int32), z_count)
    kernel = make_kernel(
        coef,
        (freq_y[:, None, None], freq_x[None, :, None], freq_z[None, None, :]),
        (y_count, x_count, z_count),
    )
    real_next = kernel[:, 0] * real_part[0] + kernel[:, 1] * real_part[1]
    imag_next = kernel[:, 0] * imag_part[0] + kernel[:, 1] * imag_part[1]
    real_part = real_next
    imag_part = imag_next
    real_part, imag_part = complex_apply(
        "bkxm,mz->bkxz", real_part, imag_part, zi_cos, zi_sin, -1.0
    )

    def relay_back(values):
        values = values.reshape(batch, ky_block, x_block, pz_count, z_local).transpose(
            0, 1, 3, 2, 4
        )
        return values.reshape(batch, ky_block, pz_count * x_block * z_local)

    real_part = relay_back(real_part)
    imag_part = relay_back(imag_part)
    real_in = lax.all_to_all(real_part, "pz", split_axis=2, concat_axis=1, tiled=True)
    imag_in = lax.all_to_all(imag_part, "pz", split_axis=2, concat_axis=1, tiled=True)
    back_items = real_in.shape[0]
    real_out, imag_out = complex_apply("bkc,ky->byc", real_in, imag_in, yi_cos, yi_sin, -1.0)

    def relay(values):
        values = values.reshape(back_items, y_count, x_block, z_local).transpose(0, 2, 1, 3)
        return values.reshape(back_items, x_block, y_count * z_local)

    real_part = relay(real_out)
    imag_part = relay(imag_out)
    real_in = lax.all_to_all(real_part, "py", split_axis=2, concat_axis=1, tiled=True)
    imag_in = lax.all_to_all(imag_part, "py", split_axis=2, concat_axis=1, tiled=True)
    result = contract("bqs,qx->bsx", real_in, xi_cos) - contract("bqs,qx->bsx", imag_in, xi_sin)
    return (
        result[0].reshape(y_local, z_local, x_count),
        result[1].reshape(y_local, z_local, x_count),
    )


def solution(mesh):
    in_specs = (P("py", "pz", None), P("py", "pz", None), P())
    out_specs = (P("py", "pz", None), P("py", "pz", None))
    return jax.shard_map(shards, mesh=mesh, in_specs=in_specs, out_specs=out_specs, check_vma=False)
```

profile of v0, /device:TPU:0, one launch (start us, length us, event | category | flops | bytes accessed | tf_op | source)
XLA Modules:
  0.0 1785.4 jit_solution(6525902035825200465)
XLA Ops:
  0.7 13.6 fusion.15
  56.9 36.3 %convolution_bitcast_fusion = f32[2,512,2048]{2,1,0:T(8,128)S(1)} fusion(f32[2,2048,512]{2,1,0:T(8,128)} %bitcast.222, s32[512]{0:T(512)S(1)} %fusion.138), kind=kOutput, calls=%fused_computation.64 | convolution fusion | flops 12888571904 | bytes 16779264 | tf_op jit(solution)/shard_map/bsx,xq->bqs/dot_general | solution.py:48
  110.0 48.6 %multiply_bitcast_fusion = f32[2,512,2048]{2,1,0:T(8,128)S(1)} fusion(f32[2,2048,512]{2,1,0:T(8,128)} %bitcast.223, s32[512]{0:T(512)S(1)} %fusion.138), kind=kOutput, calls=%fused_computation.54 | convolution fusion | flops 12890669056 | bytes 16779264 | tf_op jit(solution)/shard_map/bsx,xq->bqs/dot_general | solution.py:48
  169.8 33.0 %all-to-all-done = f32[2,512,2048]{2,0,1:T(2,128)} async-done(((f32[2,512,2048]{2,0,1:T(2,128)}), f32[2,512,2048]{2,0,1:T(2,128)}, u32[]{:S(2)}, u32[]{:S(2)}) %all-to-all-start) | async-done | bytes 8388640 | tf_op jit(solution)/shard_map/all_to_all | solution.py:94
  239.1 62.9 %all-to-all-done.1 = f32[2,512,2048]{2,0,1:T(2,128)} async-done(((f32[2,512,2048]{2,0,1:T(2,128)}), f32[2,512,2048]{2,0,1:T(2,128)}, u32[]{:S(2)}, u32[]{:S(2)}) %all-to-all-start.1) | async-done | bytes 8388640 | tf_op jit(solution)/shard_map/all_to_all | solution.py:95
  332.7 13.9 fusion.96
  346.6 11.6 add_bitcast_fusion.1
  373.3 11.7 fusion.94
  385.0 11.7 subtract_bitcast_fusion.1
  406.5 150.7 %all-to-all-done.2 = f32[2,256,4096]{2,0,1:T(2,128)} async-done(((f32[2,256,4096]{2,0,1:T(2,128)}), f32[2,256,4096]{2,0,1:T(2,128)}, u32[]{:S(2)}, u32[]{:S(2)}) %all-to-all-start.2) | async-done | bytes 8388640 | tf_op jit(solution)/shard_map/all_to_all | solution.py:105
  564.1 58.6 %fusion.10 = f32[2,2,32,128,256]{4,1,0,3,2:T(2,128)} fusion(f32[8]{0:T(128)S(1)} %add_multiply_fusion, f32[32,128,256]{2,1,0:T(8,128)S(1)} %sqrt_multiply_fusion, f32[2,2,8]{2,1,0:T(2,128)S(1)} %copy-done), kind=kOutput, calls=%fused_computation.19 | convolution fusion | flops 436207616 | bytes 20971680 | tf_op jit(solution)/shard_map/abr,rkxm->abkxm/dot_general | solution.py:67
  622.7 20.1 %fusion.246 = (f32[2,1,32,128,256]{4,1,0,3,2:T(1,128)}, f32[2,1,32,128,256]{4,1,0,3,2:T(1,128)}) fusion(f32[2,2,32,128,256]{4,1,0,3,2:T(2,128)} %fusion.10), kind=kLoop, calls=%fused_computation.302 | loop fusion | bytes 33554432 | tf_op jit(solution)/shard_map/slice | solution.py:128
  642.8 11.5 copy.249
  654.3 20.1 %reshape.291 = f32[2,32,8,128,32]{4,3,2,1,0:T(8,128)} reshape(f32[2,32,8,4096]{3,2,1,0:T(8,128)} %bitcast.231) | data formatting | bytes 16777216 | tf_op jit(solution)/shard_map/reshape | solution.py:110
  674.5 21.7 %copy.133 = f32[2,32,128,8,32]{2,4,3,1,0:T(8,128)} copy(f32[2,32,128,8,32]{4,2,3,1,0:T(8,128)} %bitcast.202) | data formatting | bytes 16777216 | tf_op jit(solution)/shard_map/transpose | solution.py:110
  696.2 19.7 %fusion.90 = f32[2,32,128,256]{3,2,1,0:T(8,128)} fusion(f32[2,32,128,256]{2,3,1,0:T(8,128)} %bitcast.212, s32[256]{0:T(256)S(1)} %compare_select_fusion.8), kind=kOutput, calls=%fused_computation.129 | convolution fusion | flops 6443368448 | bytes 16778240 | tf_op jit(solution)/shard_map/bkxz,zm->bkxm/dot_general | solution.py:48
  715.9 30.5 %all-to-all-done.3 = f32[2,256,4096]{2,0,1:T(2,128)} async-done(((f32[2,256,4096]{2,0,1:T(2,128)}), f32[2,256,4096]{2,0,1:T(2,128)}, u32[]{:S(2)}, u32[]{:S(2)}) %all-to-all-start.3) | async-done | bytes 8388640 | tf_op jit(solution)/shard_map/all_to_all | solution.py:106
  757.9 20.1 %reshape.293 = f32[2,32,8,128,32]{4,3,2,1,0:T(8,128)} reshape(f32[2,32,8,4096]{3,2,1,0:T(8,128)} %bitcast.232) | data formatting | bytes 16777216 | tf_op jit(solution)/shard_map/reshape | solution.py:110
  778.0 21.7 %copy.140 = f32[2,32,128,8,32]{2,4,3,1,0:T(8,128)} copy(f32[2,32,128,8,32]{4,2,3,1,0:T(8,128)} %bitcast.203) | data formatting | bytes 16777216 | tf_op jit(solution)/shard_map/transpose | solution.py:110
  799.7 19.4 %fusion.88 = f32[2,32,128,256]{3,2,1,0:T(8,128)S(1)} fusion(f32[2,32,128,256]{2,3,1,0:T(8,128)} %bitcast.216, s32[256]{0:T(256)S(1)} %compare_select_fusion.8), kind=kOutput, calls=%fused_computation.127 | convolution fusion | flops 6443368448 | bytes 16778240 | tf_op jit(solution)/shard_map/bkxz,zm->bkxm/dot_general | solution.py:48
  819.2 21.1 %convolution_add_fusion = f32[2,32,128,256]{3,2,1,0:T(8,128)} fusion(f32[2,32,128,256]{3,2,1,0:T(8,128)} %fusion.90, f32[2,32,128,256]{2,3,1,0:T(8,128)S(1)} %bitcast.217, s32[256]{0:T(256)S(1)} %compare_select_fusion.8), kind=kOutput, calls=%fused_computation.71 | convolution fusion | flops 6445465600 | bytes 25166848 | tf_op jit(solution)/shard_map/bkxz,zm->bkxm/dot_general | solution.py:48
  840.3 18.4 %convolution_subtract_fusion = f32[2,32,128,256]{3,2,1,0:T(8,128)} fusion(f32[2,32,128,256]{3,2,1,0:T(8,128)S(1)} %fusion.88, f32[2,32,128,256]{2,3,1,0:T(8,128)S(1)} %bitcast.215, s32[256]{0:T(256)S(1)} %compare_select_fusion.8), kind=kOutput, calls=%fused_computation.70 | convolution fusion | flops 6445465600 | bytes 25166848 | tf_op jit(solution)/shard_map/bkxz,zm->bkxm/dot_general | solution.py:48
  866.1 30.2 %fusion.27 = (f32[2,32,128,256]{3,0,2,1:T(2,128)}, f32[2,32,128,256]{3,0,2,1:T(2,128)}) fusion(f32[2,1,32,128,256]{4,1,0,3,2:T(1,128)} %get-tuple-element.5, f32[2,1,32,128,256]{4,1,0,3,2:T(1,128)} %get-tuple-element.4, f32[32,128,256]{2,1,0:T(8,128)} %get-tuple-element.20, f32[32,128,256]{2,1,0:T(8,128)} %get-tuple-element.21, ...), kind=kLoop, calls=%fused_computation.44 | loop fusion | flops 12582912 | bytes 50331648 | tf_op jit(solution)/shard_map/add | solution.py:128
  896.4 13.0 fusion.31
  929.7 28.6 %copy.203 = f32[2,32,8,128,32]{1,0,4,3,2:T(2,128)} copy(f32[2,32,8,128,32]{3,4,2,1,0:T(8,128)} %bitcast.233) | data formatting | bytes 16777216 | tf_op jit(solution)/shard_map/reshape | solution.py:140
  958.3 35.4 %reshape.323 = f32[8,1,262144]{2,1,0:T(1,128)} reshape(f32[32768,2,32]{2,1,0:T(2,128)} %bitcast.204) | data formatting | bytes 16777216
  998.9 12.4 fusion.29
  1011.3 14.5 multiply_subtract_fusion
  1034.7 28.6 %copy.208 = f32[2,32,8,128,32]{1,0,4,3,2:T(2,128)} copy(f32[2,32,8,128,32]{3,4,2,1,0:T(8,128)} %bitcast.234) | data formatting | bytes 16777216 | tf_op jit(solution)/shard_map/reshape | solution.py:140
  1063.4 35.8 %reshape.321 = f32[8,1,262144]{2,1,0:T(1,128)} reshape(f32[32768,2,32]{2,1,0:T(2,128)} %bitcast.205) | data formatting | bytes 16777216
  1099.2 83.5 %all-to-all-done.4 = f32[8,1,262144]{2,1,0:T(1,128)} async-done(((f32[8,1,262144]{2,1,0:T(1,128)}), f32[8,1,262144]{2,1,0:T(1,128)}, u32[]{:S(2)}, u32[]{:S(2)}) %all-to-all-start.4) | async-done | bytes 8388640 | tf_op jit(solution)/shard_map/all_to_all | solution.py:144
  1188.2 28.2 %reduce.1 = f32[8,262144]{1,0:T(8,128)} reduce(f32[8,1,262144]{2,1,0:T(1,128)} %all-to-all-done.4, f32[]{:T(128)} %broadcast.767), dimensions={1}, to_apply=%all_to_all.108.reduce_sub_computation | reduce | bytes 16777220 | tf_op jit(solution)/shard_map/all_to_all | solution.py:144
  1216.4 55.1 %reshape.324 = f32[32768,2,32]{2,1,0:T(2,128)} reshape(f32[8,262144]{1,0:T(8,128)} %reduce.1) | data formatting | bytes 16777216
  1271.4 40.0 %copy.205 = f32[2,32,8,4096]{3,1,2,0:T(8,128)} copy(f32[2,32,8,4096]{1,0,3,2:T(2,128)} %bitcast.206) | data formatting | bytes 16777216 | tf_op jit(solution)/shard_map/all_to_all | solution.py:144
  1311.4 60.1 %all-to-all-done.5 = f32[8,1,262144]{2,1,0:T(1,128)} async-done(((f32[8,1,262144]{2,1,0:T(1,128)}), f32[8,1,262144]{2,1,0:T(1,128)}, u32[]{:S(2)}, u32[]{:S(2)}) %all-to-all-start.5) | async-done | bytes 8388640 | tf_op jit(solution)/shard_map/all_to_all | solution.py:145
  1371.5 28.2 %reduce = f32[8,262144]{1,0:T(8,128)} reduce(f32[8,1,262144]{2,1,0:T(1,128)} %all-to-all-done.5, f32[]{:T(128)} %broadcast.767), dimensions={1}, to_apply=%all_to_all.112.reduce_sub_computation | reduce | bytes 16777220 | tf_op jit(solution)/shard_map/all_to_all | solution.py:145
  1399.7 54.9 %reshape.322 = f32[32768,2,32]{2,1,0:T(2,128)} reshape(f32[8,262144]{1,0:T(8,128)} %reduce) | data formatting | bytes 16777216
  1454.6 40.0 %copy.210 = f32[2,32,8,4096]{3,1,2,0:T(8,128)} copy(f32[2,32,8,4096]{1,0,3,2:T(2,128)} %bitcast.207) | data formatting | bytes 16777216 | tf_op jit(solution)/shard_map/all_to_all | solution.py:145
  1494.6 11.7 fusion.98
  1506.3 14.5 subtract_bitcast_fusion
  1540.9 15.4 copy.172
  1562.1 11.7 fusion.100
  1573.8 14.1 add_bitcast_fusion
  1607.9 15.7 copy.167
  1623.6 30.8 %all-to-all-done.7 = f32[2,128,8192]{1,0,2:T(2,128)} async-done(((f32[2,128,8192]{1,0,2:T(2,128)}), f32[2,128,8192]{1,0,2:T(2,128)}, u32[]{:S(2)}, u32[]{:S(2)}) %all-to-all-start.7) | async-done | bytes 8388640 | tf_op jit(solution)/shard_map/all_to_all | solution.py:156
  1664.1 20.1 %fusion.20 = f32[2,2048,512]{2,1,0:T(8,128)} fusion(f32[2,4,256,8,128]{4,3,2,1,0:T(8,128)S(1)} %bitcast.243, s32[512]{0:T(512)S(1)} %copy-done.10), kind=kOutput, calls=%fused_computation.31 | convolution fusion | flops 12888834048 | bytes 16779264 | tf_op jit(solution)/shard_map/bqs,qx->bsx/dot_general | solution.py:48
  1684.1 67.9 %all-to-all-done.6 = f32[2,128,8192]{1,0,2:T(2,128)} async-done(((f32[2,128,8192]{1,0,2:T(2,128)}), f32[2,128,8192]{1,0,2:T(2,128)}, u32[]{:S(2)}, u32[]{:S(2)}) %all-to-all-start.6) | async-done | bytes 8388640 | tf_op jit(solution)/shard_map/all_to_all | solution.py:155
  1759.7 21.1 %fusion.37 = f32[2,2048,512]{2,1,0:T(8,128)S(1)} fusion(f32[2,2048,512]{2,1,0:T(8,128)S(1)} %copy-done.7, f32[2,4,256,8,128]{4,3,2,1,0:T(8,128)} %bitcast.230, s32[512]{0:T(512)S(1)} %copy-done.10), kind=kOutput, calls=%fused_computation.69 | convolution fusion | flops 12890931200 | bytes 25167872 | tf_op jit(solution)/shard_map/bqs,qx->bsx/dot_general | solution.py:48
  (81 shorter events, 295.4 us)
Async XLA Ops:
  0.6 563.5 %copy-start = (f32[2,2,8]{2,1,0:T(2,128)S(1)}, f32[2,2,8]{2,1,0:T(2,128)}, u32[]{:S(2)}) copy-start(f32[2,2,8]{2,1,0:T(2,128)} %param.5) | copy-start | bytes 388
  0.6 13.7 copy-start.5
  0.7 13.6 copy-start.6
  25.9 8.3 collective-permute-start
  29.0 7.5 collective-permute-start.1
  37.0 8.5 collective-permute-start.2
  37.1 8.5 collective-permute-start.3
  40.6 69.3 %copy-start.9 = (s32[512]{0:T(512)}, s32[512]{0:T(512)S(1)}, u32[]{:S(2)}) copy-start(s32[512]{0:T(512)S(1)} %fusion.138) | copy-start | bytes 6148
  104.3 98.5 %all-to-all-start = ((f32[2,512,2048]{2,0,1:T(2,128)}), f32[2,512,2048]{2,0,1:T(2,128)}, u32[]{:S(2)}, u32[]{:S(2)}) async-start(f32[2,512,2048]{2,0,1:T(2,128)} %copy.120), calls=%async_computation | async-start | bytes 16777216 | tf_op jit(solution)/shard_map/all_to_all | solution.py:94
  202.8 99.2 %all-to-all-start.1 = ((f32[2,512,2048]{2,0,1:T(2,128)}), f32[2,512,2048]{2,0,1:T(2,128)}, u32[]{:S(2)}, u32[]{:S(2)}) async-start(f32[2,512,2048]{2,0,1:T(2,128)} %copy.126), calls=%async_computation.1 | async-start | bytes 16777216 | tf_op jit(solution)/shard_map/all_to_all | solution.py:95
  332.7 13.9 copy-start.3
  368.1 189.0 %all-to-all-start.2 = ((f32[2,256,4096]{2,0,1:T(2,128)}), f32[2,256,4096]{2,0,1:T(2,128)}, u32[]{:S(2)}, u32[]{:S(2)}) async-start(f32[2,256,4096]{2,0,1:T(2,128)} %copy.131), calls=%async_computation.2 | async-start | bytes 16777216 | tf_op jit(solution)/shard_map/all_to_all | solution.py:105
  557.1 189.2 %all-to-all-start.3 = ((f32[2,256,4096]{2,0,1:T(2,128)}), f32[2,256,4096]{2,0,1:T(2,128)}, u32[]{:S(2)}, u32[]{:S(2)}) async-start(f32[2,256,4096]{2,0,1:T(2,128)} %copy.138), calls=%async_computation.3 | async-start | bytes 16777216 | tf_op jit(solution)/shard_map/all_to_all | solution.py:106
  799.7 19.4 %copy-start.2 = (f32[2,32,128,8,32]{2,4,3,1,0:T(8,128)S(1)}, f32[2,32,128,8,32]{2,4,3,1,0:T(8,128)}, u32[]{:S(2)}) copy-start(f32[2,32,128,8,32]{2,4,3,1,0:T(8,128)} %copy.140) | copy-start | bytes 25165828
  799.7 40.6 %slice-start = ((s8[8388608]{0:T(1024)(128)(4,1)}), s8[4194304]{0:T(1024)(128)(4,1)S(1)}, s32[]{:S(2)}) async-start(s8[8388608]{0:T(1024)(128)(4,1)} %bitcast.213), calls=%async_computation.8 | async-start | bytes 8388608
  819.1 21.2 %slice-start.1 = ((s8[8388608]{0:T(1024)(128)(4,1)}), s8[4194304]{0:T(1024)(128)(4,1)S(1)}, s32[]{:S(2)}) async-start(s8[8388608]{0:T(1024)(128)(4,1)} %bitcast.213), calls=%async_computation.9 | async-start | bytes 8388608
  840.3 18.4 %copy-start.8 = (f32[2,32,128,256]{3,2,1,0:T(8,128)S(1)}, f32[2,32,128,256]{3,2,1,0:T(8,128)}, u32[]{:S(2)}) copy-start(f32[2,32,128,256]{3,2,1,0:T(8,128)} %convolution_add_fusion) | copy-start | bytes 25165828
  896.4 13.0 copy-start.4
  993.7 189.0 %all-to-all-start.4 = ((f32[8,1,262144]{2,1,0:T(1,128)}), f32[8,1,262144]{2,1,0:T(1,128)}, u32[]{:S(2)}, u32[]{:S(2)}) async-start(f32[8,1,262144]{2,1,0:T(1,128)} %reshape.323), calls=%async_computation.4 | async-start | bytes 16777216 | tf_op jit(solution)/shard_map/all_to_all | solution.py:144
  1182.7 188.8 %all-to-all-start.5 = ((f32[8,1,262144]{2,1,0:T(1,128)}), f32[8,1,262144]{2,1,0:T(1,128)}, u32[]{:S(2)}, u32[]{:S(2)}) async-start(f32[8,1,262144]{2,1,0:T(1,128)} %reshape.321), calls=%async_computation.5 | async-start | bytes 16777216 | tf_op jit(solution)/shard_map/all_to_all | solution.py:145
  1556.3 98.2 %all-to-all-start.7 = ((f32[2,128,8192]{1,0,2:T(2,128)}), f32[2,128,8192]{1,0,2:T(2,128)}, u32[]{:S(2)}, u32[]{:S(2)}) async-start(f32[2,128,8192]{1,0,2:T(2,128)} %copy.172), calls=%async_computation.7 | async-start | bytes 16777216 | tf_op jit(solution)/shard_map/all_to_all | solution.py:156
  1654.4 97.6 %all-to-all-start.6 = ((f32[2,128,8192]{1,0,2:T(2,128)}), f32[2,128,8192]{1,0,2:T(2,128)}, u32[]{:S(2)}, u32[]{:S(2)}) async-start(f32[2,128,8192]{1,0,2:T(2,128)} %copy.167), calls=%async_computation.6 | async-start | bytes 16777216 | tf_op jit(solution)/shard_map/all_to_all | solution.py:155
  1660.1 3.9 copy-start.10
  1752.0 7.7 copy-start.7
  1759.7 25.5 %copy-start.1 = (f32[2,2,8]{2,1,0:T(2,128)S(1)}, f32[2,2,8]{2,1,0:T(2,128)}, u32[]{:S(2)}) copy-start(f32[2,2,8]{2,1,0:T(2,128)} %param.5) | copy-start | bytes 388
where the time goes:
time: 1800 us; the launch traced here: 1790 us
  local copies, waits for them, and re-layouts  661 us (37%)
  waiting for transfers between devices  531 us (30%)
  matrix products  416 us (23%)
  other arithmetic  125 us (7%)
  starting transfers between devices  51 us (3%)
    dot_general x20, matrix products, contract(): return jnp.einsum(form, data, table, precision=HIGH)  357 us
    unnamed x30, local copies, waits for them, and re-layouts  181 us
    all_to_all x1, waiting for transfers between devices, shards(): lax.all_to_all(real_part, 'pz', split_axis=1, concat_axis=2, tiled=True)  151 us
    all_to_all x1, waiting for transfers between devices, shards(): lax.all_to_all(real_part, 'pz', split_axis=2, concat_axis=1, tiled=True)  83.5 us
    all_to_all x1, waiting for transfers between devices, shards(): lax.all_to_all(real_part, 'py', split_axis=2, concat_axis=1, tiled=True)  67.9 us
    all_to_all x1, waiting for transfers between devices, shards(): lax.all_to_all(imag_part, 'py', split_axis=1, concat_axis=2, tiled=True)  62.9 us
    all_to_all x1, waiting for transfers between devices, shards(): lax.all_to_all(imag_part, 'pz', split_axis=2, concat_axis=1, tiled=True)  60.1 us
    dot_general x1, matrix products, make_kernel(): kernel = jnp.einsum('abr,rkxm->abkxm', coef, basis, precision=HIGH)  58.6 us
  transfers between devices with their start and end apart: 12, of which 11 were waited for; matrix products, arithmetic and copies ran while one was open for 33% of the time, Pallas kernels for 0%

commit v1 on v0

--- a/solution.py
+++ b/solution.py
@@ -142,7 +142,16 @@
     real_part = relay_back(real_part)
     imag_part = relay_back(imag_part)
     real_in = lax.all_to_all(real_part, "pz", split_axis=2, concat_axis=1, tiled=True)
-    imag_in = lax.all_to_all(imag_part, "pz", split_axis=2, concat_axis=1, tiled=True)
+    replace_the_heaps = lambda x_part: jnp.concatenate(
+        lax.all_to_all(
+            jnp.stack(jnp.split(x_part, lax.psum(1, axis_name="pz"), axis=2), axis=0),
+            axis_name="pz",
+            split_axis=0,
+            concat_axis=0,
+        ),
+        axis=1,
+    )
+    imag_in = replace_the_heaps(imag_part)
     back_items = real_in.shape[0]
     real_out, imag_out = complex_apply("bkc,ky->byc", real_in, imag_in, yi_cos, yi_sin, -1.0)
 

time: 1800 us -> 1680 us (0.933)
  local copies, waits for them, and re-layouts: 661 us -> 565 us
  other arithmetic: 125 us -> 97 us
    unnamed x30 -> x41, local copies, waits for them, and re-layouts: 181 us -> 106 us
    all_to_all x2 -> x0, local copies, waits for them, and re-layouts: 40.5 us -> none  [shards(): lax.all_to_all(imag_part, 'pz', split_axis=2, concat_axis=1, tiled=True)]
    all_to_all x1 -> x0, other arithmetic: 28.2 us -> none  [shards(): lax.all_to_all(imag_part, 'pz', split_axis=2, concat_axis=1, tiled=True)]
    transpose x0 -> x1, local copies, waits for them, and re-layouts: none -> 19.6 us  [relay_back(): values.reshape(batch, ky_block, x_block, pz_count, z_local)]
    all_to_all x1 -> x2, local copies, waits for them, and re-layouts: 40 us -> 40.5 us  [shards(): lax.all_to_all(real_part, 'pz', split_axis=2, concat_axis=1, tiled=True)]
  transfers between devices with their start and end apart: 12 -> 12, of which waited for: 11 -> 11; matrix products, arithmetic and copies ran while one was open for 33% -> 35% of each run, Pallas kernels for 0% -> 0%
where the time goes in v1:
time: 1680 us; the launch traced here: 1670 us
  local copies, waits for them, and re-layouts  565 us (34%)
  waiting for transfers between devices  536 us (32%)
  matrix products  415 us (25%)
  other arithmetic  97 us (6%)
  starting transfers between devices  51 us (3%)
    dot_general x20, matrix products, contract(): return jnp.einsum(form, data, table, precision=HIGH)  357 us
    all_to_all x1, waiting for transfers between devices, shards(): lax.all_to_all(real_part, 'pz', split_axis=1, concat_axis=2, tiled=True)  151 us
    unnamed x41, local copies, waits for them, and re-layouts  106 us
    all_to_all x1, waiting for transfers between devices, shards(): lax.all_to_all(real_part, 'pz', split_axis=2, concat_axis=1, tiled=True)  88.9 us
    all_to_all x1, waiting for transfers between devices, shards(): lax.all_to_all(real_part, 'py', split_axis=2, concat_axis=1, tiled=True)  68 us
    all_to_all x1, waiting for transfers between devices, shards(): lax.all_to_all(imag_part, 'py', split_axis=1, concat_axis=2, tiled=True)  62.9 us
    all_to_all x1, waiting for transfers between devices, shards(): lax.all_to_all(jnp.stack(jnp.split(x_part, lax.psum(1, axis_name='pz'), a...  60.3 us
    dot_general x1, matrix products, make_kernel(): kernel = jnp.einsum('abr,rkxm->abkxm', coef, basis, precision=HIGH)  58.6 us
  transfers between devices with their start and end apart: 12, of which 11 were waited for; matrix products, arithmetic and copies ran while one was open for 35% of the time, Pallas kernels for 0%

profile of v1, /device:TPU:0, one launch (start us, length us, event | category | flops | bytes accessed | tf_op | source)
XLA Modules:
  0.0 1666.0 jit_solution(7886279953638968034)
XLA Ops:
  0.7 13.5 fusion.15
  56.7 36.3 %convolution_bitcast_fusion = f32[2,512,2048]{2,1,0:T(8,128)S(1)} fusion(f32[2,2048,512]{2,1,0:T(8,128)} %bitcast.250, s32[512]{0:T(512)S(1)} %fusion.146), kind=kOutput, calls=%fused_computation.64 | convolution fusion | flops 12888571904 | bytes 16779264 | tf_op jit(solution)/shard_map/bsx,xq->bqs/dot_general | solution.py:48
  109.8 48.6 %multiply_bitcast_fusion = f32[2,512,2048]{2,1,0:T(8,128)S(1)} fusion(f32[2,2048,512]{2,1,0:T(8,128)} %bitcast.251, s32[512]{0:T(512)S(1)} %fusion.146), kind=kOutput, calls=%fused_computation.54 | convolution fusion | flops 12890669056 | bytes 16779264 | tf_op jit(solution)/shard_map/bsx,xq->bqs/dot_general | solution.py:48
  169.6 33.0 %all-to-all-done = f32[2,512,2048]{2,0,1:T(2,128)} async-done(((f32[2,512,2048]{2,0,1:T(2,128)}), f32[2,512,2048]{2,0,1:T(2,128)}, u32[]{:S(2)}, u32[]{:S(2)}) %all-to-all-start) | async-done | bytes 8388640 | tf_op jit(solution)/shard_map/all_to_all | solution.py:94
  208.3 11.5 copy.126
  238.9 62.9 %all-to-all-done.1 = f32[2,512,2048]{2,0,1:T(2,128)} async-done(((f32[2,512,2048]{2,0,1:T(2,128)}), f32[2,512,2048]{2,0,1:T(2,128)}, u32[]{:S(2)}, u32[]{:S(2)}) %all-to-all-start.1) | async-done | bytes 8388640 | tf_op jit(solution)/shard_map/all_to_all | solution.py:95
  301.8 11.5 copy.132
  332.5 13.9 fusion.104
  346.5 11.6 add_bitcast_fusion.1
  373.1 11.7 fusion.102
  384.8 11.7 subtract_bitcast_fusion.1
  406.3 150.7 %all-to-all-done.2 = f32[2,256,4096]{2,0,1:T(2,128)} async-done(((f32[2,256,4096]{2,0,1:T(2,128)}), f32[2,256,4096]{2,0,1:T(2,128)}, u32[]{:S(2)}, u32[]{:S(2)}) %all-to-all-start.2) | async-done | bytes 8388640 | tf_op jit(solution)/shard_map/all_to_all | solution.py:105
  563.9 58.6 %fusion.10 = f32[2,2,32,128,256]{4,1,0,3,2:T(2,128)} fusion(f32[8]{0:T(128)S(1)} %add_multiply_fusion, f32[32,128,256]{2,1,0:T(8,128)S(1)} %sqrt_multiply_fusion, f32[2,2,8]{2,1,0:T(2,128)S(1)} %copy-done), kind=kOutput, calls=%fused_computation.19 | convolution fusion | flops 436207616 | bytes 20971680 | tf_op jit(solution)/shard_map/abr,rkxm->abkxm/dot_general | solution.py:67
  622.6 20.3 %fusion.254 = (f32[2,1,32,128,256]{4,1,0,3,2:T(1,128)}, f32[2,1,32,128,256]{4,1,0,3,2:T(1,128)}) fusion(f32[2,2,32,128,256]{4,1,0,3,2:T(2,128)} %fusion.10), kind=kLoop, calls=%fused_computation.318 | loop fusion | bytes 33554432 | tf_op jit(solution)/shard_map/slice | solution.py:128
  642.9 11.6 copy.248
  654.4 20.1 %reshape.297 = f32[2,32,8,128,32]{4,3,2,1,0:T(8,128)} reshape(f32[2,32,8,4096]{3,2,1,0:T(8,128)} %bitcast.259) | data formatting | bytes 16777216 | tf_op jit(solution)/shard_map/reshape | solution.py:110
  674.5 21.7 %copy.138 = f32[2,32,128,8,32]{2,4,3,1,0:T(8,128)} copy(f32[2,32,128,8,32]{4,2,3,1,0:T(8,128)} %bitcast.230) | data formatting | bytes 16777216 | tf_op jit(solution)/shard_map/transpose | solution.py:110
  696.3 19.7 %fusion.98 = f32[2,32,128,256]{3,2,1,0:T(8,128)} fusion(f32[2,32,128,256]{2,3,1,0:T(8,128)} %bitcast.238, s32[256]{0:T(256)S(1)} %compare_select_fusion.8), kind=kOutput, calls=%fused_computation.145 | convolution fusion | flops 6443368448 | bytes 16778240 | tf_op jit(solution)/shard_map/bkxz,zm->bkxm/dot_general | solution.py:48
  716.0 30.2 %all-to-all-done.3 = f32[2,256,4096]{2,0,1:T(2,128)} async-done(((f32[2,256,4096]{2,0,1:T(2,128)}), f32[2,256,4096]{2,0,1:T(2,128)}, u32[]{:S(2)}, u32[]{:S(2)}) %all-to-all-start.3) | async-done | bytes 8388640 | tf_op jit(solution)/shard_map/all_to_all | solution.py:106
  746.2 11.5 copy.247
  757.7 20.1 %reshape.299 = f32[2,32,8,128,32]{4,3,2,1,0:T(8,128)} reshape(f32[2,32,8,4096]{3,2,1,0:T(8,128)} %bitcast.260) | data formatting | bytes 16777216 | tf_op jit(solution)/shard_map/reshape | solution.py:110
  777.8 21.7 %copy.145 = f32[2,32,128,8,32]{2,4,3,1,0:T(8,128)} copy(f32[2,32,128,8,32]{4,2,3,1,0:T(8,128)} %bitcast.231) | data formatting | bytes 16777216 | tf_op jit(solution)/shard_map/transpose | solution.py:110
  799.5 19.5 %fusion.96 = f32[2,32,128,256]{3,2,1,0:T(8,128)S(1)} fusion(f32[2,32,128,256]{2,3,1,0:T(8,128)} %bitcast.242, s32[256]{0:T(256)S(1)} %compare_select_fusion.8), kind=kOutput, calls=%fused_computation.143 | convolution fusion | flops 6443368448 | bytes 16778240 | tf_op jit(solution)/shard_map/bkxz,zm->bkxm/dot_general | solution.py:48
  819.0 21.1 %convolution_add_fusion = f32[2,32,128,256]{3,2,1,0:T(8,128)} fusion(f32[2,32,128,256]{3,2,1,0:T(8,128)} %fusion.98, f32[2,32,128,256]{2,3,1,0:T(8,128)S(1)} %bitcast.243, s32[256]{0:T(256)S(1)} %compare_select_fusion.8), kind=kOutput, calls=%fused_computation.71 | convolution fusion | flops 6445465600 | bytes 25166848 | tf_op jit(solution)/shard_map/bkxz,zm->bkxm/dot_general | solution.py:48
  840.1 18.4 %convolution_subtract_fusion = f32[2,32,128,256]{3,2,1,0:T(8,128)} fusion(f32[2,32,128,256]{3,2,1,0:T(8,128)S(1)} %fusion.96, f32[2,32,128,256]{2,3,1,0:T(8,128)S(1)} %bitcast.241, s32[256]{0:T(256)S(1)} %compare_select_fusion.8), kind=kOutput, calls=%fused_computation.70 | convolution fusion | flops 6445465600 | bytes 25166848 | tf_op jit(solution)/shard_map/bkxz,zm->bkxm/dot_general | solution.py:48
  866.0 30.3 %fusion.27 = (f32[2,32,128,256]{3,0,2,1:T(2,128)}, f32[2,32,128,256]{3,0,2,1:T(2,128)}) fusion(f32[2,1,32,128,256]{4,1,0,3,2:T(1,128)} %get-tuple-element.5, f32[2,1,32,128,256]{4,1,0,3,2:T(1,128)} %get-tuple-element.4, f32[32,128,256]{2,1,0:T(8,128)} %get-tuple-element.20, f32[32,128,256]{2,1,0:T(8,128)} %get-tuple-element.21, ...), kind=kLoop, calls=%fused_computation.44 | loop fusion | flops 12582912 | bytes 50331648 | tf_op jit(solution)/shard_map/add | solution.py:128
  896.3 13.0 fusion.31
  929.5 28.7 %copy.206 = f32[2,32,8,128,32]{1,0,4,3,2:T(2,128)} copy(f32[2,32,8,128,32]{3,4,2,1,0:T(8,128)} %bitcast.261) | data formatting | bytes 16777216 | tf_op jit(solution)/shard_map/reshape | solution.py:140
  958.2 35.4 %reshape.329 = f32[8,1,262144]{2,1,0:T(1,128)} reshape(f32[32768,2,32]{2,1,0:T(2,128)} %bitcast.232) | data formatting | bytes 16777216
  998.7 12.4 fusion.29
  1011.1 14.5 multiply_subtract_fusion
  1034.6 19.6 %copy.166 = f32[2,32,8,128,32]{4,3,2,1,0:T(8,128)} copy(f32[2,32,8,128,32]{3,4,2,1,0:T(8,128)} %bitcast.262) | data formatting | bytes 16777216 | tf_op jit(solution)/shard_map/transpose | solution.py:137
  1054.2 21.2 %reshape.304 = f32[2,32,32768]{2,1,0:T(8,128)} reshape(f32[2,32,8,128,32]{4,3,2,1,0:T(8,128)} %copy.166) | data formatting | bytes 16777216 | tf_op jit(solution)/shard_map/reshape | solution.py:140
  1093.7 88.9 %all-to-all-done.4 = f32[8,1,262144]{2,1,0:T(1,128)} async-done(((f32[8,1,262144]{2,1,0:T(1,128)}), f32[8,1,262144]{2,1,0:T(1,128)}, u32[]{:S(2)}, u32[]{:S(2)}) %all-to-all-start.4) | async-done | bytes 8388640 | tf_op jit(solution)/shard_map/all_to_all | solution.py:144
  1188.1 28.2 %reduce = f32[8,262144]{1,0:T(8,128)} reduce(f32[8,1,262144]{2,1,0:T(1,128)} %all-to-all-done.4, f32[]{:T(128)} %broadcast.767), dimensions={1}, to_apply=%all_to_all.98.reduce_sub_computation | reduce | bytes 16777220 | tf_op jit(solution)/shard_map/all_to_all | solution.py:144
  1216.3 54.9 %reshape.330 = f32[32768,2,32]{2,1,0:T(2,128)} reshape(f32[8,262144]{1,0:T(8,128)} %reduce) | data formatting | bytes 16777216
  1271.1 40.0 %copy.208 = f32[2,32,8,4096]{3,1,2,0:T(8,128)} copy(f32[2,32,8,4096]{1,0,3,2:T(2,128)} %bitcast.233) | data formatting | bytes 16777216 | tf_op jit(solution)/shard_map/all_to_all | solution.py:144
  1311.1 60.3 %all-to-all-done.5 = f32[8,2,32,4096]{3,2,1,0:T(8,128)} async-done(((f32[8,2,32,4096]{3,2,1,0:T(8,128)}), f32[8,2,32,4096]{3,2,1,0:T(8,128)}, u32[]{:S(2)}, u32[]{:S(2)}) %all-to-all-start.5) | async-done | bytes 8388640 | tf_op jit(solution)/shard_map/all_to_all | solution.py:146
  1375.5 11.4 fusion.106
  1387.0 14.5 subtract_bitcast_fusion
  1421.5 15.4 copy.175
  1442.7 11.7 fusion.108
  1454.5 14.1 add_bitcast_fusion
  1488.6 15.6 copy.170
  1504.3 30.8 %all-to-all-done.7 = f32[2,128,8192]{1,0,2:T(2,128)} async-done(((f32[2,128,8192]{1,0,2:T(2,128)}), f32[2,128,8192]{1,0,2:T(2,128)}, u32[]{:S(2)}, u32[]{:S(2)}) %all-to-all-start.7) | async-done | bytes 8388640 | tf_op jit(solution)/shard_map/all_to_all | solution.py:165
  1544.7 19.9 %fusion.20 = f32[2,2048,512]{2,1,0:T(8,128)} fusion(f32[2,4,256,8,128]{4,3,2,1,0:T(8,128)S(1)} %bitcast.271, s32[512]{0:T(512)S(1)} %copy-done.11), kind=kOutput, calls=%fused_computation.31 | convolution fusion | flops 12888834048 | bytes 16779264 | tf_op jit(solution)/shard_map/bqs,qx->bsx/dot_general | solution.py:48
  1564.6 68.0 %all-to-all-done.6 = f32[2,128,8192]{1,0,2:T(2,128)} async-done(((f32[2,128,8192]{1,0,2:T(2,128)}), f32[2,128,8192]{1,0,2:T(2,128)}, u32[]{:S(2)}, u32[]{:S(2)}) %all-to-all-start.6) | async-done | bytes 8388640 | tf_op jit(solution)/shard_map/all_to_all | solution.py:164
  1640.3 21.1 %fusion.37 = f32[2,2048,512]{2,1,0:T(8,128)S(1)} fusion(f32[2,2048,512]{2,1,0:T(8,128)S(1)} %copy-done.8, f32[2,4,256,8,128]{4,3,2,1,0:T(8,128)} %bitcast.258, s32[512]{0:T(512)S(1)} %copy-done.11), kind=kOutput, calls=%fused_computation.69 | convolution fusion | flops 12890931200 | bytes 25167872 | tf_op jit(solution)/shard_map/bqs,qx->bsx/dot_general | solution.py:48
  (94 shorter events, 283.2 us)
Async XLA Ops:
  0.6 563.3 %copy-start = (f32[2,2,8]{2,1,0:T(2,128)S(1)}, f32[2,2,8]{2,1,0:T(2,128)}, u32[]{:S(2)}) copy-start(f32[2,2,8]{2,1,0:T(2,128)} %param.5) | copy-start | bytes 388
  0.6 13.5 copy-start.6
  0.7 13.5 copy-start.7
  25.8 8.3 collective-permute-start
  28.8 7.5 collective-permute-start.1
  36.9 8.5 collective-permute-start.2
  36.9 8.5 collective-permute-start.3
  40.5 69.3 %copy-start.10 = (s32[512]{0:T(512)}, s32[512]{0:T(512)S(1)}, u32[]{:S(2)}) copy-start(s32[512]{0:T(512)S(1)} %fusion.146) | copy-start | bytes 6148
  104.1 98.5 %all-to-all-start = ((f32[2,512,2048]{2,0,1:T(2,128)}), f32[2,512,2048]{2,0,1:T(2,128)}, u32[]{:S(2)}, u32[]{:S(2)}) async-start(f32[2,512,2048]{2,0,1:T(2,128)} %copy.125), calls=%async_computation | async-start | bytes 16777216 | tf_op jit(solution)/shard_map/all_to_all | solution.py:94
  202.6 99.2 %all-to-all-start.1 = ((f32[2,512,2048]{2,0,1:T(2,128)}), f32[2,512,2048]{2,0,1:T(2,128)}, u32[]{:S(2)}, u32[]{:S(2)}) async-start(f32[2,512,2048]{2,0,1:T(2,128)} %copy.131), calls=%async_computation.1 | async-start | bytes 16777216 | tf_op jit(solution)/shard_map/all_to_all | solution.py:95
  332.5 13.9 copy-start.4
  367.9 189.0 %all-to-all-start.2 = ((f32[2,256,4096]{2,0,1:T(2,128)}), f32[2,256,4096]{2,0,1:T(2,128)}, u32[]{:S(2)}, u32[]{:S(2)}) async-start(f32[2,256,4096]{2,0,1:T(2,128)} %copy.136), calls=%async_computation.2 | async-start | bytes 16777216 | tf_op jit(solution)/shard_map/all_to_all | solution.py:105
  557.0 189.2 %all-to-all-start.3 = ((f32[2,256,4096]{2,0,1:T(2,128)}), f32[2,256,4096]{2,0,1:T(2,128)}, u32[]{:S(2)}, u32[]{:S(2)}) async-start(f32[2,256,4096]{2,0,1:T(2,128)} %copy.143), calls=%async_computation.3 | async-start | bytes 16777216 | tf_op jit(solution)/shard_map/all_to_all | solution.py:106
  799.5 19.5 %copy-start.2 = (f32[2,32,128,8,32]{2,4,3,1,0:T(8,128)S(1)}, f32[2,32,128,8,32]{2,4,3,1,0:T(8,128)}, u32[]{:S(2)}) copy-start(f32[2,32,128,8,32]{2,4,3,1,0:T(8,128)} %copy.145) | copy-start | bytes 25165828
  799.5 40.6 %slice-start.2 = ((s8[8388608]{0:T(1024)(128)(4,1)}), s8[4194304]{0:T(1024)(128)(4,1)S(1)}, s32[]{:S(2)}) async-start(s8[8388608]{0:T(1024)(128)(4,1)} %bitcast.239), calls=%async_computation.10 | async-start | bytes 8388608
  819.0 21.1 %slice-start.3 = ((s8[8388608]{0:T(1024)(128)(4,1)}), s8[4194304]{0:T(1024)(128)(4,1)S(1)}, s32[]{:S(2)}) async-start(s8[8388608]{0:T(1024)(128)(4,1)} %bitcast.239), calls=%async_computation.11 | async-start | bytes 8388608
  840.1 18.4 %copy-start.9 = (f32[2,32,128,256]{3,2,1,0:T(8,128)S(1)}, f32[2,32,128,256]{3,2,1,0:T(8,128)}, u32[]{:S(2)}) copy-start(f32[2,32,128,256]{3,2,1,0:T(8,128)} %convolution_add_fusion) | copy-start | bytes 25165828
  896.2 13.0 copy-start.5
  993.6 189.0 %all-to-all-start.4 = ((f32[8,1,262144]{2,1,0:T(1,128)}), f32[8,1,262144]{2,1,0:T(1,128)}, u32[]{:S(2)}, u32[]{:S(2)}) async-start(f32[8,1,262144]{2,1,0:T(1,128)} %reshape.329), calls=%async_computation.4 | async-start | bytes 16777216 | tf_op jit(solution)/shard_map/all_to_all | solution.py:144
  1182.6 188.8 %all-to-all-start.5 = ((f32[8,2,32,4096]{3,2,1,0:T(8,128)}), f32[8,2,32,4096]{3,2,1,0:T(8,128)}, u32[]{:S(2)}, u32[]{:S(2)}) async-start(f32[8,2,32,4096]{3,2,1,0:T(8,128)} %fusion.52), calls=%async_computation.5 | async-start | bytes 16777216 | tf_op jit(solution)/shard_map/all_to_all | solution.py:146
  1371.4 15.6 slice-start
  1375.5 11.5 copy-start.3
  1375.5 11.5 slice-start.1
  1436.9 98.1 %all-to-all-start.7 = ((f32[2,128,8192]{1,0,2:T(2,128)}), f32[2,128,8192]{1,0,2:T(2,128)}, u32[]{:S(2)}, u32[]{:S(2)}) async-start(f32[2,128,8192]{1,0,2:T(2,128)} %copy.175), calls=%async_computation.7 | async-start | bytes 16777216 | tf_op jit(solution)/shard_map/all_to_all | solution.py:165
  1535.0 97.6 %all-to-all-start.6 = ((f32[2,128,8192]{1,0,2:T(2,128)}), f32[2,128,8192]{1,0,2:T(2,128)}, u32[]{:S(2)}, u32[]{:S(2)}) async-start(f32[2,128,8192]{1,0,2:T(2,128)} %copy.170), calls=%async_computation.6 | async-start | bytes 16777216 | tf_op jit(solution)/shard_map/all_to_all | solution.py:164
  1540.7 3.9 copy-start.11
  1632.6 7.7 copy-start.8
  1640.3 25.5 %copy-start.1 = (f32[2,2,8]{2,1,0:T(2,128)S(1)}, f32[2,2,8]{2,1,0:T(2,128)}, u32[]{:S(2)}) copy-start(f32[2,2,8]{2,1,0:T(2,128)} %param.5) | copy-start | bytes 388
